TPU v7x, 512 devices: a whole 4x8x8 slice. The times are simulated.
512 devices in a mesh: gx: 32 (over x, z), gy: 8 (over y_lo, core), phys: 2 (over y_hi).
Axes of the slice: x: 4, y: 8 (y_hi: 2, y_lo: 4; y = y_hi * 4 + y_lo), z: 8, core: 2. Of those that a mesh axis runs over, the one named last changes fastest.
Arguments:
- mech_load: float32 [32, 8, 2, 128, 768], P('gx', 'gy', 'phys'), may hold values from -63 to 63
- heat_load: float32 [32, 8, 2, 128, 256], P('gx', 'gy', 'phys'), may hold values from -63 to 63
- mech_factor: bfloat16 [32, 8, 2, 768, 768], P('gx', 'gy', 'phys'), may hold values from -0.21875 to 0.21875
- heat_factor: bfloat16 [32, 8, 2, 256, 256], P('gx', 'gy', 'phys'), may hold values from -0.375 to 0.375
- mech_diag: float32 [32, 8, 2, 768], P('gx', 'gy', 'phys'), may hold values from 0.1 to 1
- heat_diag: float32 [32, 8, 2, 256], P('gx', 'gy', 'phys'), may hold values from 0.1 to 1
- mech_wx: float32 [32, 8, 2, 768], P('gx', 'gy', 'phys'), may hold values from 0.5 to 4
- mech_wy: float32 [32, 8, 2, 768], P('gx', 'gy', 'phys'), may hold values from 0.5 to 4
- mech_wp: float32 [32, 8, 768], P('gx', 'gy'), may hold values from 0.5 to 4
- heat_wx: float32 [32, 8, 2, 256], P('gx', 'gy', 'phys'), may hold values from 0.5 to 4
- heat_wy: float32 [32, 8, 2, 256], P('gx', 'gy', 'phys'), may hold values from 0.5 to 4
- heat_wp: float32 [32, 8, 256], P('gx', 'gy'), may hold values from 0.5 to 4
- coupling: bfloat16 [32, 8, 2, 768, 256], P('gx', 'gy', 'phys'), may hold values from -0.21875 to 0.21875
- mech_sens: bfloat16 [32, 8, 2, 768, 256], P('gx', 'gy', 'phys'), may hold values from -0.21875 to 0.21875
- heat_sens: bfloat16 [32, 8, 2, 256, 256], P('gx', 'gy', 'phys'), may hold values from -0.375 to 0.375
- density: float32 [32, 8, 256], P('gx', 'gy', 'phys'), may hold values from 0.2 to 1
- material_ids: int32 [32, 8, 256], P('gx', 'gy', 'phys'), may hold values from 0 to 7
- material_scale: float32 [8], replicated, may hold values from 1 to 10
Outputs:
- mech_adjoint: float32 [32, 8, 2, 128, 768], P('gx', 'gy', 'phys')
- heat_adjoint: float32 [32, 8, 2, 128, 256], P('gx', 'gy', 'phys')
- gradient: float32 [32, 8, 256], P('gx', 'gy', 'phys')
All inputs are finite; a program needn't handle non-finite values.
Results may differ from a plain program's by a relative error of at most 0.014.
Values may be sent and summed in bfloat16 or wider, within the bound.
A program may use at most 64 MiB of HBM per device.

v0:
```python
import jax
import jax.numpy as jnp
from jax import lax
from jax.sharding import PartitionSpec as P

LOADS = 128
ITERS = 2


def with_halo(array, sides, width):
    for axis, dim in sides:
        devices, length = (lax.axis_size(axis), array.shape[dim])
        up = [(i, (i + 1) % devices) for i in range(devices - 1)]
        down = [(j, i) for i, j in up]
        last = lax.slice_in_dim(array, length - width, length, axis=dim)
        initial = lax.slice_in_dim(array, 0, width, axis=dim)
        before = lax.ppermute(last, axis, up)
        after = lax.ppermute(initial, axis, down)
        array = jnp.concatenate([before, array, after], axis=dim)
    return array


def from_partner(array, axis, apart):
    return lax.ppermute(array, axis, [(i, i ^ 1 << apart) for i in range(lax.axis_size(axis))])


def from_behind(array, axis, by):
    devices = lax.axis_size(axis)
    pairs = [(i, i + by) for i in range(devices) if 0 <= i + by < devices]
    return lax.ppermute(array, axis, pairs)


def apply_operator(rounded, coefs, thermal):
    factor, diagonal, lower_x, upper_x, lower_y, upper_y, partner_weight = coefs
    block = rounded[None, None, None]
    if thermal:
        padded = with_halo(block, (("gx", 0), ("gy", 1)), 1)
        partner = from_partner(rounded, "phys", 0)
    else:
        padded = with_halo(block, (("gx", 0), ("gy", 1)), 1)
        partner = from_partner(rounded, "phys", 0)
    middle = 0
    western = padded[0, 1, middle].astype(jnp.float32)
    eastern = padded[2, 1, middle].astype(jnp.float32)
    southern = padded[1, 0, middle].astype(jnp.float32)
    northern = padded[1, 2, middle].astype(jnp.float32)
    inner = jnp.dot(rounded, factor, preferred_element_type=jnp.float32).astype(jnp.bfloat16)
    schur = lax.dot_general(
        inner, factor, (((1,), (1,)), ((), ())), preferred_element_type=jnp.float32
    )
    values = rounded.astype(jnp.float32)
    image = schur + diagonal * values
    image = image + lower_x * (values - western) + upper_x * (values - eastern)
    image = image + lower_y * (values - southern) + upper_y * (values - northern)
    image = image + partner_weight * (values - partner.astype(jnp.float32))
    return image


def interface_solve(load, coefs, thermal):
    solution = jnp.zeros_like(load)
    residual = load
    direction = load
    if thermal:
        current = lax.psum(jnp.sum(load * load, axis=1), ("gx", "gy", "phys"))
    else:
        current = lax.psum(jnp.sum(load * load, axis=1), ("gx", "gy", "phys"))
    for iteration in range(ITERS):
        rounded = direction.astype(jnp.bfloat16)
        image = apply_operator(rounded, coefs, thermal)
        local_curv = jnp.sum(rounded.astype(jnp.float32) * image, axis=1)
        if thermal:
            curvature = lax.psum(local_curv, ("gx", "gy", "phys"))
        else:
            curvature = lax.psum(local_curv, ("gx", "gy", "phys"))
        alpha = current / curvature
        solution = solution + alpha[:, None] * direction
        if iteration + 1 < ITERS:
            residual = residual - alpha[:, None] * image
            if thermal:
                following = lax.psum(jnp.sum(residual * residual, axis=1), ("gx", "gy", "phys"))
            else:
                following = lax.psum(jnp.sum(residual * residual, axis=1), ("gx", "gy", "phys"))
            direction = residual + (following / current)[:, None] * direction
            current = following
    return solution


def on_device(
    mech_load,
    heat_load,
    mech_factor,
    heat_factor,
    mech_diag,
    heat_diag,
    mech_wx,
    mech_wy,
    mech_wp,
    heat_wx,
    heat_wy,
    heat_wp,
    coupling,
    mech_sens,
    heat_sens,
    density,
    material_ids,
    material_scale,
):
    mech_width = mech_load.shape[-1]
    lower_rows = jnp.concatenate([mech_wx[0, 0, 0], heat_wx[0, 0, 0]])
    lower_cols = jnp.concatenate([mech_wy[0, 0, 0], heat_wy[0, 0, 0]])
    upper_rows = from_behind(lower_rows, "gx", -1)
    upper_cols = from_behind(lower_cols, "gy", -1)
    mech_coefs = (
        mech_factor[0, 0, 0],
        mech_diag[0, 0, 0],
        mech_wx[0, 0, 0],
        upper_rows[:mech_width],
        mech_wy[0, 0, 0],
        upper_cols[:mech_width],
        mech_wp[0, 0],
    )
    mech_adjoint = interface_solve(mech_load[0, 0, 0], mech_coefs, False)
    coupled = jnp.dot(
        mech_adjoint.astype(jnp.bfloat16), coupling[0, 0, 0], preferred_element_type=jnp.float32
    )
    heat_source = heat_load[0, 0, 0] - coupled
    heat_coefs = (
        heat_factor[0, 0, 0],
        heat_diag[0, 0, 0],
        heat_wx[0, 0, 0],
        upper_rows[mech_width:],
        heat_wy[0, 0, 0],
        upper_cols[mech_width:],
        heat_wp[0, 0],
    )
    heat_adjoint = interface_solve(heat_source, heat_coefs, True)
    mech_energy = jnp.sum(mech_adjoint * mech_adjoint, axis=0).astype(jnp.bfloat16)
    heat_energy = jnp.sum(heat_adjoint * heat_adjoint, axis=0).astype(jnp.bfloat16)
    partial_sens = jnp.dot(mech_energy, mech_sens[0, 0, 0], preferred_element_type=jnp.float32)
    partial_sens = partial_sens + jnp.dot(
        heat_energy, heat_sens[0, 0, 0], preferred_element_type=jnp.float32
    )
    summed = lax.psum(partial_sens, "phys")
    stride = partial_sens.shape[0] // lax.axis_size("phys")
    portion = lax.dynamic_slice_in_dim(summed, lax.axis_index("phys") * stride, stride, 0)
    onehot = (
        material_ids[0, 0][:, None] == jnp.arange(material_scale.shape[0], dtype=jnp.int32)[None, :]
    ).astype(jnp.float32)
    stiffness = jnp.dot(onehot, material_scale, precision=lax.Precision.HIGHEST)
    densities = density[0, 0]
    gradient = -3.0 * densities * densities * stiffness * portion / LOADS
    return (mech_adjoint[None, None, None], heat_adjoint[None, None, None], gradient[None, None])


def solution(mesh):
    placed = (
        P("gx", "gy", "phys", None, None),
        P("gx", "gy", "phys", None, None),
        P("gx", "gy", "phys", None, None),
        P("gx", "gy", "phys", None, None),
        P("gx", "gy", "phys", None),
        P("gx", "gy", "phys", None),
        P("gx", "gy", "phys", None),
        P("gx", "gy", "phys", None),
        P("gx", "gy", None),
        P("gx", "gy", "phys", None),
        P("gx", "gy", "phys", None),
        P("gx", "gy", None),
        P("gx", "gy", "phys", None, None),
        P("gx", "gy", "phys", None, None),
        P("gx", "gy", "phys", None, None),
        P("gx", "gy", "phys"),
        P("gx", "gy", "phys"),
        P(),
    )
    return jax.shard_map(
        on_device,
        mesh=mesh,
        in_specs=placed,
        out_specs=(
            P("gx", "gy", "phys", None, None),
            P("gx", "gy", "phys", None, None),
            P("gx", "gy", "phys"),
        ),
        check_vma=False,
    )
```

profile of v0, /device:TPU:1, one launch (start us, length us, event | category | flops | bytes accessed | tf_op | source)
XLA Modules:
  0.0 722.6 jit_solution(3888469934136934606)
XLA Ops:
  2.0 4.8 collective-permute-start
  9.4 4.5 collective-permute-done.2
  13.9 5.9 collective-permute-start.3
  19.8 2.0 collective-permute-start.5
  23.8 6.5 collective-permute-start.6
  31.9 3.9 collective-permute-done.1
  36.2 2.0 fusion.30
  38.1 107.8 %all-reduce.1 = (f32[128]{0:T(128)S(1)}, f32[128]{0:T(128)S(1)}) all-reduce(f32[128]{0:T(128)S(1)} %fusion.44, f32[128]{0:T(128)S(1)} %get-tuple-element.15), channel_id=1, replica_groups=mesh['gx'=32,'gy'=8,'phys'=2] {'gx','gy','phys'}, use_global_device_ids=true, to_apply=%region_1.0 | all-reduce | flops 256 | bytes 2048 | tf_op jit(solution)/shard_map/psum | solution.py:66
  146.1 94.5 %psum.65 = f32[128]{0:T(128)S(1)} all-reduce(f32[128]{0:T(128)S(1)} %multiply_reduce_fusion.1), channel_id=1, replica_groups=mesh['gx'=32,'gy'=8,'phys'=2] {'gx','gy','phys'}, use_global_device_ids=true, to_apply=%region_5.0 | all-reduce | flops 128 | bytes 1024 | tf_op jit(solution)/shard_map/psum | solution.py:82
  240.8 2.7 collective-permute-start.7
  244.8 2.2 collective-permute-done.7
  247.1 3.8 collective-permute-done.8
  250.9 3.8 collective-permute-start.10
  254.7 1.9 collective-permute-start.9
  256.7 4.7 collective-permute-start.11
  262.1 11.8 %collective-permute-done.11 = bf16[128,768]{1,0:T(8,128)(2,1)} collective-permute-done((bf16[128,768]{1,0:T(8,128)(2,1)S(1)}, bf16[128,768]{1,0:T(8,128)(2,1)}, u32[]{:S(2)}, u32[]{:S(2)}) %collective-permute-start.11) | collective-permute-done | bytes 196640 | tf_op jit(solution)/shard_map/ppermute | solution.py:24
  275.6 98.5 %psum.66 = f32[128]{0:T(128)S(1)} all-reduce(f32[128]{0:T(128)S(1)} %fusion.47), channel_id=1, replica_groups=mesh['gx'=32,'gy'=8,'phys'=2] {'gx','gy','phys'}, use_global_device_ids=true, to_apply=%region_7.0 | all-reduce | flops 128 | bytes 1024 | tf_op jit(solution)/shard_map/psum | solution.py:74
  374.7 3.4 collective-permute-start.12
  379.4 3.7 collective-permute-done.13
  383.1 2.9 collective-permute-start.14
  386.1 2.4 collective-permute-start.15
  388.5 4.4 collective-permute-start.16
  394.3 3.8 collective-permute-done.16
  399.6 99.2 %all-reduce = (f32[128]{0:T(128)S(1)}, f32[128]{0:T(128)S(1)}) all-reduce(f32[128]{0:T(128)S(1)} %get-tuple-element.13, f32[128]{0:T(128)S(1)} %get-tuple-element.18), channel_id=1, replica_groups=mesh['gx'=32,'gy'=8,'phys'=2] {'gx','gy','phys'}, use_global_device_ids=true, to_apply=%region_9.0 | all-reduce | flops 256 | bytes 2048 | tf_op jit(solution)/shard_map/psum | solution.py:64
  499.0 95.5 %psum.69 = f32[128]{0:T(128)S(1)} all-reduce(f32[128]{0:T(128)S(1)} %multiply_reduce_fusion.3), channel_id=1, replica_groups=mesh['gx'=32,'gy'=8,'phys'=2] {'gx','gy','phys'}, use_global_device_ids=true, to_apply=%region_13.0 | all-reduce | flops 128 | bytes 1024 | tf_op jit(solution)/shard_map/psum | solution.py:80
  594.6 3.3 collective-permute-start.17
  599.3 4.6 collective-permute-start.21
  603.9 2.1 collective-permute-start.19
  606.0 2.3 collective-permute-start.20
  609.4 3.6 collective-permute-done.20
  613.4 99.8 %psum.70 = f32[128]{0:T(128)S(1)} all-reduce(f32[128]{0:T(128)S(1)} %fusion.85), channel_id=1, replica_groups=mesh['gx'=32,'gy'=8,'phys'=2] {'gx','gy','phys'}, use_global_device_ids=true, to_apply=%region_15.0 | all-reduce | flops 128 | bytes 1024 | tf_op jit(solution)/shard_map/psum | solution.py:72
  714.1 7.7 %psum.71 = f32[256]{0:T(256)S(1)} all-reduce(f32[256]{0:T(256)S(1)} %add.136), channel_id=1, replica_groups=mesh['gx'=32,'gy'=8,'phys'=2] {'phys'}, use_global_device_ids=true, to_apply=%region_18.0 | all-reduce | flops 256 | bytes 2048 | tf_op jit(solution)/shard_map/psum | solution.py:143
  (115 shorter events, 21.3 us)
Async XLA Ops:
  2.0 7.4 %collective-permute-start = (bf16[1,1,1,128,768]{4,3,2,1,0:T(8,128)(2,1)S(1)}, bf16[1,1,1,128,768]{4,3,2,1,0:T(8,128)(2,1)S(1)}, u32[]{:S(2)}, u32[]{:S(2)}) collective-permute-start(bf16[1,1,1,128,768]{4,3,2,1,0:T(8,128)(2,1)S(1)} %get-tuple-element.11), channel_id=1, source_target_pairs={{0,16},{16,32},{32,48},{48,64},{64,80},{80,96},{96,112},{112,128},... | collective-permute-start | bytes 589832 | tf_op jit(solution)/shard_map/ppermute | solution.py:17
  6.8 7.0 collective-permute-start.2
  13.9 22.2 %collective-permute-start.3 = (bf16[3,1,1,128,768]{4,3,2,1,0:T(8,128)(2,1)S(1)}, bf16[3,1,1,128,768]{4,3,2,1,0:T(8,128)(2,1)}, u32[]{:S(2)}, u32[]{:S(2)}) collective-permute-start(bf16[3,1,1,128,768]{4,3,2,1,0:T(8,128)(2,1)S(1)} %pad_maximum_fusion), channel_id=1, source_target_pairs={{0,2},{2,4},{4,6},{6,8},{8,10},{10,12},{12,14},{1,3},{3,5},{5,7},{... | collective-permute-start | bytes 1769480 | tf_op jit(solution)/shard_map/ppermute | solution.py:17
  19.8 16.3 %collective-permute-start.5 = (bf16[3,1,1,128,768]{4,3,2,1,0:T(8,128)(2,1)S(1)}, bf16[3,1,1,128,768]{4,3,2,1,0:T(8,128)(2,1)}, u32[]{:S(2)}, u32[]{:S(2)}) collective-permute-start(bf16[3,1,1,128,768]{4,3,2,1,0:T(8,128)(2,1)S(1)} %pad_maximum_fusion), channel_id=1, source_target_pairs={{2,0},{4,2},{6,4},{8,6},{10,8},{12,10},{14,12},{3,1},{5,3},{7,5},{... | collective-permute-start | bytes 1769480 | tf_op jit(solution)/shard_map/ppermute | solution.py:18
  21.9 10.0 %collective-permute-start.4 = (f32[1024]{0:T(1024)S(1)}, f32[1024]{0:T(1024)S(1)}, u32[]{:S(2)}, u32[]{:S(2)}) collective-permute-start(f32[1024]{0:T(1024)S(1)} %pad_maximum_fusion.5), channel_id=1, source_target_pairs={{2,0},{4,2},{6,4},{8,6},{10,8},{12,10},{14,12},{3,1},{5,3},{7,5},{... | collective-permute-start | bytes 12296 | tf_op jit(solution)/shard_map/ppermute | solution.py:30
  23.8 12.3 %collective-permute-start.6 = (bf16[128,768]{1,0:T(8,128)(2,1)S(1)}, bf16[128,768]{1,0:T(8,128)(2,1)}, u32[]{:S(2)}, u32[]{:S(2)}) collective-permute-start(bf16[128,768]{1,0:T(8,128)(2,1)S(1)} %get-tuple-element.12), channel_id=1, source_target_pairs={{0,1},{1,0},{2,3},{3,2},{4,5},{5,4},{6,7},{7,6},{8,9},{9,8},{10,11... | collective-permute-start | bytes 589832 | tf_op jit(solution)/shard_map/ppermute | solution.py:24
  30.4 5.4 collective-permute-start.1
  31.9 215.2 %copy-start.7 = (f32[1024]{0:T(1024)}, f32[1024]{0:T(1024)S(1)}, u32[]{:S(2)}) copy-start(f32[1024]{0:T(1024)S(1)} %collective-permute-done.4) | copy-start | bytes 12292
  35.8 211.3 %copy-start.8 = (f32[1024]{0:T(1024)}, f32[1024]{0:T(1024)S(1)}, u32[]{:S(2)}) copy-start(f32[1024]{0:T(1024)S(1)} %collective-permute-done.1) | copy-start | bytes 12292
  145.9 101.1 %copy-start.9 = (f32[128]{0:T(128)}, f32[128]{0:T(128)S(1)}, u32[]{:S(2)}) copy-start(f32[128]{0:T(128)S(1)} %div.24) | copy-start | bytes 1540
  240.8 6.3 collective-permute-start.7
  243.5 7.3 %collective-permute-start.8 = (bf16[1,1,1,128,768]{4,3,2,1,0:T(8,128)(2,1)S(1)}, bf16[1,1,1,128,768]{4,3,2,1,0:T(8,128)(2,1)S(1)}, u32[]{:S(2)}, u32[]{:S(2)}) collective-permute-start(bf16[1,1,1,128,768]{4,3,2,1,0:T(8,128)(2,1)S(1)} %bitcast.187), channel_id=1, source_target_pairs={{16,0},{32,16},{48,32},{64,48},{80,64},{96,80},{112,96},{128,112},... | collective-permute-start | bytes 589832 | tf_op jit(solution)/shard_map/ppermute | solution.py:18
  250.9 23.0 %collective-permute-start.10 = (bf16[3,1,1,128,768]{4,3,2,1,0:T(8,128)(2,1)S(1)}, bf16[3,1,1,128,768]{4,3,2,1,0:T(8,128)(2,1)}, u32[]{:S(2)}, u32[]{:S(2)}) collective-permute-start(bf16[3,1,1,128,768]{4,3,2,1,0:T(8,128)(2,1)S(1)} %pad_maximum_fusion.1), channel_id=1, source_target_pairs={{2,0},{4,2},{6,4},{8,6},{10,8},{12,10},{14,12},{3,1},{5,3},{7,5},{... | collective-permute-start | bytes 1769480 | tf_op jit(solution)/shard_map/ppermute | solution.py:18
  254.7 19.2 %collective-permute-start.9 = (bf16[3,1,1,128,768]{4,3,2,1,0:T(8,128)(2,1)S(1)}, bf16[3,1,1,128,768]{4,3,2,1,0:T(8,128)(2,1)}, u32[]{:S(2)}, u32[]{:S(2)}) collective-permute-start(bf16[3,1,1,128,768]{4,3,2,1,0:T(8,128)(2,1)S(1)} %pad_maximum_fusion.1), channel_id=1, source_target_pairs={{0,2},{2,4},{4,6},{6,8},{8,10},{10,12},{12,14},{1,3},{3,5},{5,7},{... | collective-permute-start | bytes 1769480 | tf_op jit(solution)/shard_map/ppermute | solution.py:17
  256.7 17.3 %collective-permute-start.11 = (bf16[128,768]{1,0:T(8,128)(2,1)S(1)}, bf16[128,768]{1,0:T(8,128)(2,1)}, u32[]{:S(2)}, u32[]{:S(2)}) collective-permute-start(bf16[128,768]{1,0:T(8,128)(2,1)S(1)} %fusion.48), channel_id=1, source_target_pairs={{0,1},{1,0},{2,3},{3,2},{4,5},{5,4},{6,7},{7,6},{8,9},{9,8},{10,11... | collective-permute-start | bytes 589832 | tf_op jit(solution)/shard_map/ppermute | solution.py:24
  262.1 112.0 %copy-start.10 = (f32[128]{0:T(128)S(1)}, f32[128]{0:T(128)}, u32[]{:S(2)}) copy-start(f32[128]{0:T(128)} %copy-done.9) | copy-start | bytes 1540
  374.7 233.7 %copy-start.3 = (bf16[1,1,1,768,256]{4,3,2,1,0:T(8,128)(2,1)S(1)}, bf16[1,1,1,768,256]{4,3,2,1,0:T(8,128)(2,1)}, u32[]{:S(2)}) copy-start(bf16[1,1,1,768,256]{4,3,2,1,0:T(8,128)(2,1)} %param.31) | copy-start | bytes 1179652
  374.7 4.7 collective-permute-start.12
  378.1 5.0 collective-permute-start.13
  383.1 14.9 %collective-permute-start.14 = (bf16[3,1,1,128,256]{4,3,2,1,0:T(8,128)(2,1)S(1)}, bf16[3,1,1,128,256]{4,3,2,1,0:T(8,128)(2,1)S(1)}, u32[]{:S(2)}, u32[]{:S(2)}) collective-permute-start(bf16[3,1,1,128,256]{4,3,2,1,0:T(8,128)(2,1)S(1)} %pad_maximum_fusion.2), channel_id=1, source_target_pairs={{0,2},{2,4},{4,6},{6,8},{8,10},{10,12},{12,14},{1,3},{3,5},{5,7},{... | collective-permute-start | bytes 589832 | tf_op jit(solution)/shard_map/ppermute | solution.py:17
  386.1 12.0 %collective-permute-start.15 = (bf16[3,1,1,128,256]{4,3,2,1,0:T(8,128)(2,1)S(1)}, bf16[3,1,1,128,256]{4,3,2,1,0:T(8,128)(2,1)S(1)}, u32[]{:S(2)}, u32[]{:S(2)}) collective-permute-start(bf16[3,1,1,128,256]{4,3,2,1,0:T(8,128)(2,1)S(1)} %pad_maximum_fusion.2), channel_id=1, source_target_pairs={{2,0},{4,2},{6,4},{8,6},{10,8},{12,10},{14,12},{3,1},{5,3},{7,5},{... | collective-permute-start | bytes 589832 | tf_op jit(solution)/shard_map/ppermute | solution.py:18
  388.5 9.6 %collective-permute-start.16 = (bf16[128,256]{1,0:T(8,128)(2,1)S(1)}, bf16[128,256]{1,0:T(8,128)(2,1)S(1)}, u32[]{:S(2)}, u32[]{:S(2)}) collective-permute-start(bf16[128,256]{1,0:T(8,128)(2,1)S(1)} %get-tuple-element.14), channel_id=1, source_target_pairs={{0,1},{1,0},{2,3},{3,2},{4,5},{5,4},{6,7},{7,6},{8,9},{9,8},{10,11... | collective-permute-start | bytes 196616 | tf_op jit(solution)/shard_map/ppermute | solution.py:24
  398.1 214.9 %copy-start.21 = (bf16[1,1,1,256,256]{4,3,2,1,0:T(8,128)(2,1)S(1)}, bf16[1,1,1,256,256]{4,3,2,1,0:T(8,128)(2,1)}, u32[]{:S(2)}) copy-start(bf16[1,1,1,256,256]{4,3,2,1,0:T(8,128)(2,1)} %param.21) | copy-start | bytes 393220
  594.6 119.4 %copy-start.5 = (bf16[1,1,1,256,256]{4,3,2,1,0:T(8,128)(2,1)S(1)}, bf16[1,1,1,256,256]{4,3,2,1,0:T(8,128)(2,1)}, u32[]{:S(2)}) copy-start(bf16[1,1,1,256,256]{4,3,2,1,0:T(8,128)(2,1)} %param.32) | copy-start | bytes 393220
  594.6 9.3 %collective-permute-start.17 = (bf16[1,1,1,128,256]{4,3,2,1,0:T(8,128)(2,1)S(1)}, bf16[1,1,1,128,256]{4,3,2,1,0:T(8,128)(2,1)S(1)}, u32[]{:S(2)}, u32[]{:S(2)}) collective-permute-start(bf16[1,1,1,128,256]{4,3,2,1,0:T(8,128)(2,1)S(1)} %bitcast.190), channel_id=1, source_target_pairs={{0,16},{16,32},{32,48},{48,64},{64,80},{80,96},{96,112},{112,128},... | collective-permute-start | bytes 196616 | tf_op jit(solution)/shard_map/ppermute | solution.py:17
  597.9 6.0 collective-permute-start.18
  599.2 122.6 %copy-start.24 = (s32[1,1,128]{2,1,0:T(1,128)S(1)}, s32[1,1,128]{2,1,0:T(1,128)}, u32[]{:S(2)}) copy-start(s32[1,1,128]{2,1,0:T(1,128)} %param.34) | copy-start | bytes 1540
  599.2 122.6 %copy-start.25 = (f32[8]{0:T(128)S(1)}, f32[8]{0:T(128)}, u32[]{:S(2)}) copy-start(f32[8]{0:T(128)} %param.35) | copy-start | bytes 100
  599.2 122.5 %copy-start.26 = (f32[1,1,128]{2,1,0:T(1,128)S(1)}, f32[1,1,128]{2,1,0:T(1,128)}, u32[]{:S(2)}) copy-start(f32[1,1,128]{2,1,0:T(1,128)} %param.33) | copy-start | bytes 1540
  599.3 9.2 %collective-permute-start.21 = (bf16[128,256]{1,0:T(8,128)(2,1)S(1)}, bf16[128,256]{1,0:T(8,128)(2,1)S(1)}, u32[]{:S(2)}, u32[]{:S(2)}) collective-permute-start(bf16[128,256]{1,0:T(8,128)(2,1)S(1)} %fusion.86), channel_id=1, source_target_pairs={{0,1},{1,0},{2,3},{3,2},{4,5},{5,4},{6,7},{7,6},{8,9},{9,8},{10,11... | collective-permute-start | bytes 196616 | tf_op jit(solution)/shard_map/ppermute | solution.py:24
  603.9 5.5 collective-permute-start.19
  606.0 7.0 collective-permute-start.20
  (19 other events, 765.4 us)
where the time goes:
time: 724 us; the launch traced here: 723 us
  blocking collectives  603 us (83%)
  starting transfers between devices  66.2 us (9%)
  waiting for transfers between devices  39.9 us (6%)
    psum x2, blocking collectives, interface_solve(): current = lax.psum(jnp.sum(load * load, axis=1), ('gx', 'gy', 'phys'))  207 us
    psum x2, blocking collectives, interface_solve(): curvature = lax.psum(local_curv, ('gx', 'gy', 'phys'))  198 us
    psum x2, blocking collectives, interface_solve(): lax.psum(jnp.sum(residual * residual, axis=1), ('gx', 'gy', 'phys'))  190 us
    ppermute x8, starting transfers between devices, with_halo(): before = lax.ppermute(last, axis, up)  27.1 us
    ppermute x4, starting transfers between devices, from_partner(): lax.ppermute(array, axis, [(i, i ^ 1 << apart) for i in range(lax.axis_si...  20.2 us
    ppermute x4, waiting for transfers between devices, from_partner(): lax.ppermute(array, axis, [(i, i ^ 1 << apart) for i in range(lax.axis_si...  16 us
    ppermute x8, starting transfers between devices, with_halo(): after = lax.ppermute(initial, axis, down)  15.7 us
    ppermute x8, waiting for transfers between devices, with_halo(): after = lax.ppermute(initial, axis, down)  15.5 us
  transfers between devices with their start and end apart: 22, of which 11 were waited for; matrix products, arithmetic and copies ran while one was open for 0% of the time, Pallas kernels for 0%

commit v1 on v0

--- a/solution.py
+++ b/solution.py
@@ -69,7 +69,7 @@
         image = apply_operator(rounded, coefs, thermal)
         local_curv = jnp.sum(rounded.astype(jnp.float32) * image, axis=1)
         if thermal:
-            curvature = lax.psum(local_curv, ("gx", "gy", "phys"))
+            curvature = jnp.sum(lax.all_gather(local_curv, ("gx", "gy", "phys")), axis=0)
         else:
             curvature = lax.psum(local_curv, ("gx", "gy", "phys"))
         alpha = current / curvature

time: 724 us -> 3090 us (4.27)
  blocking collectives: 603 us -> 2970 us
    all_gather x0 -> x2, blocking collectives: none -> 2470 us  [interface_solve(): lax.all_gather(local_curv, ('gx', 'gy', 'phys'))]
    psum x2 -> x1, blocking collectives: 198 us -> 98.5 us  [interface_solve(): curvature = lax.psum(local_curv, ('gx', 'gy', 'phys'))]
  transfers between devices with their start and end apart: 22 -> 22, of which waited for: 11 -> 10; matrix products, arithmetic and copies ran while one was open for 0% -> 0% of each run, Pallas kernels for 0% -> 0%
where the time goes in v1:
time: 3090 us; the launch traced here: 3080 us
  blocking collectives  2970 us (96%)
  starting transfers between devices  65 us (2%)
  waiting for transfers between devices  36.4 us (1%)
    all_gather x2, blocking collectives, interface_solve(): lax.all_gather(local_curv, ('gx', 'gy', 'phys'))  2470 us
    psum x2, blocking collectives, interface_solve(): current = lax.psum(jnp.sum(load * load, axis=1), ('gx', 'gy', 'phys'))  208 us
    psum x2, blocking collectives, interface_solve(): lax.psum(jnp.sum(residual * residual, axis=1), ('gx', 'gy', 'phys'))  189 us
    psum x1, blocking collectives, interface_solve(): curvature = lax.psum(local_curv, ('gx', 'gy', 'phys'))  98.5 us
  transfers between devices with their start and end apart: 22, of which 10 were waited for; matrix products, arithmetic and copies ran while one was open for 0% of the time, Pallas kernels for 0%

profile of v1, /device:TPU:1, one launch (start us, length us, event | category | flops | bytes accessed | tf_op | source)
XLA Modules:
  0.0 3084.3 jit_solution(2373056938076089766)
XLA Ops:
  2.0 4.8 collective-permute-start
  9.4 4.5 collective-permute-done.2
  13.9 5.9 collective-permute-start.3
  19.8 2.0 collective-permute-start.5
  23.8 6.5 collective-permute-start.6
  31.9 3.9 collective-permute-done.1
  36.2 2.0 fusion.30
  38.1 107.8 %all-reduce = (f32[128]{0:T(128)S(1)}, f32[128]{0:T(128)S(1)}) all-reduce(f32[128]{0:T(128)S(1)} %fusion.44, f32[128]{0:T(128)S(1)} %get-tuple-element.13), channel_id=1, replica_groups=mesh['gx'=32,'gy'=8,'phys'=2] {'gx','gy','phys'}, use_global_device_ids=true, to_apply=%region_1.0 | all-reduce | flops 256 | bytes 2048 | tf_op jit(solution)/shard_map/psum | solution.py:66
  146.1 94.5 %psum.51 = f32[128]{0:T(128)S(1)} all-reduce(f32[128]{0:T(128)S(1)} %multiply_reduce_fusion.1), channel_id=1, replica_groups=mesh['gx'=32,'gy'=8,'phys'=2] {'gx','gy','phys'}, use_global_device_ids=true, to_apply=%region_5.0 | all-reduce | flops 128 | bytes 1024 | tf_op jit(solution)/shard_map/psum | solution.py:82
  240.8 2.7 collective-permute-start.7
  244.8 2.2 collective-permute-done.7
  247.1 3.8 collective-permute-done.8
  250.9 3.8 collective-permute-start.10
  254.7 1.9 collective-permute-start.9
  256.7 4.7 collective-permute-start.11
  262.1 11.8 collective-permute-done.11
  275.6 98.5 %psum.52 = f32[128]{0:T(128)S(1)} all-reduce(f32[128]{0:T(128)S(1)} %fusion.47), channel_id=1, replica_groups=mesh['gx'=32,'gy'=8,'phys'=2] {'gx','gy','phys'}, use_global_device_ids=true, to_apply=%region_7.0 | all-reduce | flops 128 | bytes 1024 | tf_op jit(solution)/shard_map/psum | solution.py:74
  374.7 3.2 collective-permute-start.12
  379.3 3.7 collective-permute-done.13
  383.0 2.9 collective-permute-start.14
  385.9 2.4 collective-permute-start.15
  388.3 4.4 collective-permute-start.16
  394.1 99.9 %psum.53 = f32[128]{0:T(128)S(1)} all-reduce(f32[128]{0:T(128)S(1)} %get-tuple-element.11), channel_id=1, replica_groups=mesh['gx'=32,'gy'=8,'phys'=2] {'gx','gy','phys'}, use_global_device_ids=true, to_apply=%region_9.0 | all-reduce | flops 128 | bytes 1024 | tf_op jit(solution)/shard_map/psum | solution.py:64
  494.6 1234.1 %all-gather.2 = f32[512,1,128]{2,1,0:T(1,128)S(1)} all-gather(f32[1,1,128]{2,1,0:T(1,128)S(1)} %bitcast.211), channel_id=2, replica_groups=mesh['gx'=32,'gy'=8,'phys'=2] {'gx','gy','phys'}, dimensions={0}, use_global_device_ids=true | all-gather | bytes 262656 | tf_op jit(solution)/shard_map/all_gather | solution.py:72
  1729.4 94.2 %psum.54 = f32[128]{0:T(128)S(1)} all-reduce(f32[128]{0:T(128)S(1)} %multiply_reduce_fusion.3), channel_id=1, replica_groups=mesh['gx'=32,'gy'=8,'phys'=2] {'gx','gy','phys'}, use_global_device_ids=true, to_apply=%region_13.0 | all-reduce | flops 128 | bytes 1024 | tf_op jit(solution)/shard_map/psum | solution.py:80
  1823.6 2.0 collective-permute-start.17
  1827.0 4.7 collective-permute-start.21
  1831.8 2.5 collective-permute-start.19
  1834.3 2.1 collective-permute-start.20
  1837.6 3.7 collective-permute-done.20
  1841.7 1232.7 %all-gather.3 = f32[512,1,128]{2,1,0:T(1,128)S(1)} all-gather(f32[1,1,128]{2,1,0:T(1,128)S(1)} %bitcast.212), channel_id=3, replica_groups=mesh['gx'=32,'gy'=8,'phys'=2] {'gx','gy','phys'}, dimensions={0}, use_global_device_ids=true | all-gather | bytes 262656 | tf_op jit(solution)/shard_map/all_gather | solution.py:72
  3075.9 7.7 psum.55
  (120 shorter events, 21.5 us)
Async XLA Ops:
  2.0 7.4 collective-permute-start
  6.8 7.0 collective-permute-start.2
  13.9 22.2 collective-permute-start.3
  19.8 16.3 collective-permute-start.5
  21.9 10.0 collective-permute-start.4
  23.8 12.3 collective-permute-start.6
  30.4 5.4 collective-permute-start.1
  31.9 215.2 %copy-start.7 = (f32[1024]{0:T(1024)}, f32[1024]{0:T(1024)S(1)}, u32[]{:S(2)}) copy-start(f32[1024]{0:T(1024)S(1)} %collective-permute-done.4) | copy-start | bytes 12292
  35.8 211.3 %copy-start.8 = (f32[1024]{0:T(1024)}, f32[1024]{0:T(1024)S(1)}, u32[]{:S(2)}) copy-start(f32[1024]{0:T(1024)S(1)} %collective-permute-done.1) | copy-start | bytes 12292
  240.8 6.3 collective-permute-start.7
  243.5 7.3 collective-permute-start.8
  250.9 23.0 collective-permute-start.10
  254.7 19.2 collective-permute-start.9
  256.7 17.3 collective-permute-start.11
  374.1 120.0 %copy-start.18 = (f32[1,1,1,256]{3,2,1,0:T(1,128)S(1)}, f32[1,1,1,256]{3,2,1,0:T(1,128)}, u32[]{:S(2)}) copy-start(f32[1,1,1,256]{3,2,1,0:T(1,128)} %param.28) | copy-start | bytes 3076
  374.3 120.2 %copy-start.2 = (f32[128,768]{1,0:T(8,128)}, f32[128,768]{1,0:T(8,128)S(1)}, u32[]{:S(2)}) copy-start(f32[128,768]{1,0:T(8,128)S(1)} %get-tuple-element.8) | copy-start | bytes 1179652
  374.7 4.6 collective-permute-start.12
  378.0 5.0 collective-permute-start.13
  383.0 111.1 %collective-permute-start.14 = (bf16[3,1,1,128,256]{4,3,2,1,0:T(8,128)(2,1)S(1)}, bf16[3,1,1,128,256]{4,3,2,1,0:T(8,128)(2,1)S(1)}, u32[]{:S(2)}, u32[]{:S(2)}) collective-permute-start(bf16[3,1,1,128,256]{4,3,2,1,0:T(8,128)(2,1)S(1)} %pad_maximum_fusion.2), channel_id=1, source_target_pairs={{0,2},{2,4},{4,6},{6,8},{8,10},{10,12},{12,14},{1,3},{3,5},{5,7},{... | collective-permute-start | bytes 589832 | tf_op jit(solution)/shard_map/ppermute | solution.py:17
  385.9 108.1 %collective-permute-start.15 = (bf16[3,1,1,128,256]{4,3,2,1,0:T(8,128)(2,1)S(1)}, bf16[3,1,1,128,256]{4,3,2,1,0:T(8,128)(2,1)S(1)}, u32[]{:S(2)}, u32[]{:S(2)}) collective-permute-start(bf16[3,1,1,128,256]{4,3,2,1,0:T(8,128)(2,1)S(1)} %pad_maximum_fusion.2), channel_id=1, source_target_pairs={{2,0},{4,2},{6,4},{8,6},{10,8},{12,10},{14,12},{3,1},{5,3},{7,5},{... | collective-permute-start | bytes 589832 | tf_op jit(solution)/shard_map/ppermute | solution.py:18
  388.3 105.7 %collective-permute-start.16 = (bf16[128,256]{1,0:T(8,128)(2,1)S(1)}, bf16[128,256]{1,0:T(8,128)(2,1)S(1)}, u32[]{:S(2)}, u32[]{:S(2)}) collective-permute-start(bf16[128,256]{1,0:T(8,128)(2,1)S(1)} %get-tuple-element.12), channel_id=1, source_target_pairs={{0,1},{1,0},{2,3},{3,2},{4,5},{5,4},{6,7},{7,6},{8,9},{9,8},{10,11... | collective-permute-start | bytes 196616 | tf_op jit(solution)/shard_map/ppermute | solution.py:24
  494.1 1342.3 %copy-start.3 = (bf16[1,1,1,768,256]{4,3,2,1,0:T(8,128)(2,1)S(1)}, bf16[1,1,1,768,256]{4,3,2,1,0:T(8,128)(2,1)}, u32[]{:S(2)}) copy-start(bf16[1,1,1,768,256]{4,3,2,1,0:T(8,128)(2,1)} %param.31) | copy-start | bytes 1179652
  494.5 1346.8 %copy-start.22 = (bf16[1,1,1,256,256]{4,3,2,1,0:T(8,128)(2,1)S(1)}, bf16[1,1,1,256,256]{4,3,2,1,0:T(8,128)(2,1)}, u32[]{:S(2)}) copy-start(bf16[1,1,1,256,256]{4,3,2,1,0:T(8,128)(2,1)} %param.21) | copy-start | bytes 393220
  1823.6 8.1 collective-permute-start.17
  1825.7 6.1 collective-permute-start.18
  1827.0 9.6 collective-permute-start.21
  1831.8 1244.0 %copy-start.5 = (bf16[1,1,1,256,256]{4,3,2,1,0:T(8,128)(2,1)S(1)}, bf16[1,1,1,256,256]{4,3,2,1,0:T(8,128)(2,1)}, u32[]{:S(2)}) copy-start(bf16[1,1,1,256,256]{4,3,2,1,0:T(8,128)(2,1)} %param.32) | copy-start | bytes 393220
  1831.8 1251.8 %copy-start.25 = (s32[1,1,128]{2,1,0:T(1,128)S(1)}, s32[1,1,128]{2,1,0:T(1,128)}, u32[]{:S(2)}) copy-start(s32[1,1,128]{2,1,0:T(1,128)} %param.34) | copy-start | bytes 1540
  1831.8 1251.8 %copy-start.26 = (f32[8]{0:T(128)S(1)}, f32[8]{0:T(128)}, u32[]{:S(2)}) copy-start(f32[8]{0:T(128)} %param.35) | copy-start | bytes 100
  1831.8 1251.8 %copy-start.27 = (f32[1,1,128]{2,1,0:T(1,128)S(1)}, f32[1,1,128]{2,1,0:T(1,128)}, u32[]{:S(2)}) copy-start(f32[1,1,128]{2,1,0:T(1,128)} %param.33) | copy-start | bytes 1540
  1831.8 5.8 collective-permute-start.19
  1834.3 7.0 collective-permute-start.20
  (20 other events, 1337.2 us)
